TPU v7x, 128 devices: a whole 4x4x4 slice. The times are simulated.
128 devices in a mesh: sample: 4 (over z), marker: 32 (over y, x, core).
Axes of the slice: x: 4, y: 4, z: 4, core: 2. Of those that a mesh axis runs over, the one named last changes fastest.
Arguments:
- genotypes: bfloat16 [8192, 131072], P('sample', 'marker'), may hold values from -6 to 6
- phenotypes: float32 [16, 8192], P(None, 'sample'), may hold values from -6 to 6
- message: float32 [16, 131072], P(None, 'marker'), may hold values from -6 to 6
- probes: float32 [112, 131072], P(None, 'marker'), may hold values from -16 to 16
- inclusion: float32 [16], replicated, may hold values from 0.3 to 0.6
- slab_ratio: float32 [16], replicated, may hold values from 0.25 to 0.67
- input_precision: float32 [16], replicated, may hold values from 0.5 to 2
- noise_precision: float32 [16], replicated, may hold values from 4 to 16
Outputs:
- estimate: float32 [16, 131072], P(None, 'marker')
- lmmse_estimate: float32 [16, 131072], P(None, 'marker')
All inputs are finite; a program needn't handle non-finite values.
Results may differ from a plain program's by a relative error of at most 0.0013.
Values may be sent and summed in bfloat16 or wider, within the bound.
A program may use at most 128 MiB of HBM per device.

v0:
```python
import jax
import jax.numpy as jnp
from jax import lax
from jax.sharding import PartitionSpec as P

MARKERS = 131072
ITERS = 2


def denoise(signal, precision, shrink, logit_base):
    energy = shrink * precision * signal * signal
    weight = jax.nn.sigmoid(logit_base + 0.5 * energy)
    return (shrink * weight * signal, shrink * weight * (1.0 + (1.0 - weight) * energy))


def contract_rows(vectors, genotypes):
    return lax.dot_general(
        vectors, genotypes, (((1,), (1,)), ((), ())), preferred_element_type=jnp.float32
    )


def project(vectors_b, genotypes, offset):
    partial_value = contract_rows(vectors_b, genotypes)
    predicted = lax.psum(partial_value, "marker")
    if offset is not None:
        predicted = offset - predicted
    predicted_b = predicted.astype(jnp.bfloat16)
    widened = predicted_b.astype(jnp.float32)
    back_sum = jnp.dot(predicted_b, genotypes, preferred_element_type=jnp.float32)
    return (back_sum, jnp.sum(widened * widened, axis=1))


def per_device(
    genotypes, phenotypes, message, probes, inclusion, slab_ratio, input_precision, noise_precision
):
    people = genotypes.shape[0] * lax.axis_size("sample")
    traits = message.shape[0]
    copies = probes.shape[0] // traits + 1
    shrink = (slab_ratio / (1.0 + slab_ratio))[:, None]
    odds = jnp.log(inclusion / (1.0 - inclusion))[:, None]
    logit_base = odds + 0.5 * jnp.log(1.0 - shrink)
    first, slopes = denoise(message, input_precision[:, None], shrink, logit_base)
    first_slope = lax.psum(jnp.sum(slopes, axis=1), "marker") / MARKERS
    second_precision = input_precision * (1.0 - first_slope) / first_slope
    centre = (first - first_slope[:, None] * message) / (1.0 - first_slope)[:, None]
    start_back, unused_square = project(centre.astype(jnp.bfloat16), genotypes, phenotypes)
    start_back = lax.psum(start_back, "sample")
    start_res = noise_precision[:, None] / people * start_back
    scale_col = jnp.tile(noise_precision / people, copies)[:, None]
    prec_col = jnp.tile(second_precision, copies)[:, None]
    iterate = jnp.concatenate([centre, jnp.zeros(probes.shape, jnp.float32)], axis=0)
    residual = jnp.concatenate([start_res, probes], axis=0)
    direction = residual
    norm_start = lax.psum(jnp.sum(residual * residual, axis=1), "marker")
    norm_now = norm_start
    for iteration in range(ITERS):
        back_sum, square = project(direction.astype(jnp.bfloat16), genotypes, None)
        back_sum = lax.psum(back_sum, "sample")
        applied = scale_col * back_sum + prec_col * direction
        curvature = lax.psum(jnp.sum(direction * applied, axis=1), "marker")
        step_size = norm_now / curvature
        iterate = iterate + step_size[:, None] * direction
        if iteration + 1 < ITERS:
            residual = residual - step_size[:, None] * applied
            norm_next = lax.psum(jnp.sum(residual * residual, axis=1), "marker")
            beta_ratio = norm_next / norm_now
            direction = residual + beta_ratio[:, None] * direction
            norm_now = norm_next
    lmmse_estimate = iterate[:traits]
    probe_local = jnp.sum(
        jnp.sum(probes * iterate[traits:], axis=1).reshape(copies - 1, traits), axis=0
    )
    probe_dot = lax.psum(probe_local, "marker")
    probe_norm = jnp.sum(norm_start[traits:].reshape(copies - 1, traits), axis=0)
    second_slope = second_precision * probe_dot / (probe_norm + 1e-06)
    next_precision = second_precision * (1.0 - second_slope) / second_slope
    next_message = (lmmse_estimate - second_slope[:, None] * centre) / (1.0 - second_slope)[:, None]
    slab_var = slab_ratio / input_precision
    next_shrink = (slab_var * next_precision / (1.0 + slab_var * next_precision))[:, None]
    next_base = odds + 0.5 * jnp.log(1.0 - next_shrink)
    estimate, unused_slopes = denoise(next_message, next_precision[:, None], next_shrink, next_base)
    return (estimate, lmmse_estimate)


def solution(mesh):
    return jax.shard_map(
        per_device,
        mesh=mesh,
        in_specs=(
            P("sample", "marker"),
            P(None, "sample"),
            P(None, "marker"),
            P(None, "marker"),
            P(),
            P(),
            P(),
            P(),
        ),
        out_specs=(P(None, "marker"), P(None, "marker")),
        check_vma=False,
    )
```

profile of v0, /device:TPU:1, one launch (start us, length us, event | category | flops | bytes accessed | tf_op | source)
XLA Modules:
  0.0 946.0 jit_solution(1127837189394486947)
XLA Ops:
  7.2 0.7 multiply_add_fusion.4
  7.9 0.7 mul.192
  8.6 1.3 multiply_reduce_fusion.4
  9.8 63.8 %psum.84 = f32[16]{0:T(128)S(1)} all-reduce(f32[16]{0:T(128)S(1)} %multiply_reduce_fusion.4), channel_id=1, replica_groups=mesh['sample'=4,'marker'=32] {'marker'}, use_global_device_ids=true, to_apply=%region_1.0 | all-reduce | flops 16 | bytes 128 | tf_op jit(solution)/shard_map/psum | solution.py:43
  73.6 0.7 multiply_divide_fusion.1
  74.3 1.1 subtract_divide_fusion
  75.4 10.9 %fusion.17 = f32[16,2048]{1,0:T(8,128)} fusion(bf16[2048,4096]{1,0:T(8,128)(2,1)} %param.8, f32[16,4096]{1,0:T(8,128)S(1)} %subtract_divide_fusion), kind=kOutput, calls=%fused_computation.33 | convolution fusion | flops 268500992 | bytes 17170432 | tf_op jit(solution)/shard_map/dot_general | solution.py:17
  86.4 102.7 %all-reduce.9.cloned.1.call-done = f32[16,2048]{1,0:T(8,128)} async-done(((f32[16,2048]{1,0:T(8,128)}), f32[16,2048]{1,0:T(8,128)}) %all-reduce.9.cloned.1.call-update) | async-done | bytes 131088 | tf_op jit(solution)/shard_map/psum | solution.py:24
  189.1 8.8 fusion.19
  198.0 39.8 %all-reduce.11.cloned.1.call-done = f32[16,4096]{1,0:T(8,128)} async-done(((f32[16,4096]{1,0:T(8,128)}), f32[16,4096]{1,0:T(8,128)}) %all-reduce.11.cloned.1.call-update) | async-done | bytes 262160 | tf_op jit(solution)/shard_map/psum | solution.py:47
  237.8 1.0 broadcast_multiply_fusion
  238.8 11.4 %fusion.3 = f32[128,2048]{1,0:T(8,128)S(1)} fusion(bf16[2048,4096]{1,0:T(8,128)(2,1)} %param.8, f32[112,4096]{1,0:T(8,128)S(1)} %copy-done, f32[16,4096]{1,0:T(8,128)S(1)} %broadcast_multiply_fusion), kind=kOutput, calls=%fused_computation.13 | convolution fusion | flops 2149580800 | bytes 19922944 | tf_op jit(solution)/shard_map/dot_general | solution.py:17
  250.2 134.0 %all-reduce.16 = bf16[128,2048]{1,0:T(8,128)(2,1)} all-reduce(f32[128,2048]{1,0:T(8,128)S(1)} %fusion.3), channel_id=1, replica_groups=mesh['sample'=4,'marker'=32] {'marker'}, use_global_device_ids=true, to_apply=%region_6.0 | all-reduce | flops 262144 | bytes 1572864 | tf_op jit(solution)/shard_map/psum | solution.py:24
  384.2 9.6 %fusion.24 = f32[128,4096]{1,0:T(8,128)} fusion(bf16[128,2048]{1,0:T(8,128)(2,1)} %all-reduce.16, bf16[2048,4096]{1,0:T(8,128)(2,1)} %param.8), kind=kOutput, calls=%fused_computation.52 | convolution fusion | flops 2147483648 | bytes 19398656 | tf_op jit(solution)/shard_map/dot_general | solution.py:29
  394.0 0.1 mul.207
  394.1 59.5 %all-reduce.13.cloned.1.call-done = f32[128,4096]{1,0:T(8,128)} async-done(((f32[128,4096]{1,0:T(8,128)}), f32[128,4096]{1,0:T(8,128)}) %all-reduce.13.cloned.1.call-update) | async-done | bytes 2097168 | tf_op jit(solution)/shard_map/psum | solution.py:58
  453.6 2.2 multiply_reduce_fusion.2
  455.8 62.9 %all-reduce.1 = (f32[128]{0:T(128)S(1)}, f32[128]{0:T(128)S(1)}) all-reduce(f32[128]{0:T(128)S(1)} %get-tuple-element.3, f32[128]{0:T(128)S(1)} %get-tuple-element.2), channel_id=1, replica_groups=mesh['sample'=4,'marker'=32] {'marker'}, use_global_device_ids=true, to_apply=%region_5.0 | all-reduce | flops 256 | bytes 2048 | tf_op jit(solution)/shard_map/psum | solution.py:54
  518.7 2.2 multiply_reduce_fusion.1
  520.9 66.8 %psum.91 = f32[128]{0:T(128)S(1)} all-reduce(f32[128]{0:T(128)S(1)} %multiply_reduce_fusion.1), channel_id=1, replica_groups=mesh['sample'=4,'marker'=32] {'marker'}, use_global_device_ids=true, to_apply=%region_11.0 | all-reduce | flops 128 | bytes 1024 | tf_op jit(solution)/shard_map/psum | solution.py:65
  587.7 3.6 multiply_add_fusion.1
  591.3 12.1 %fusion.1 = f32[128,2048]{1,0:T(8,128)S(1)} fusion(bf16[2048,4096]{1,0:T(8,128)(2,1)} %param.8, f32[128,4096]{1,0:T(8,128)} %multiply_add_fusion.1), kind=kOutput, calls=%fused_computation.11 | convolution fusion | flops 2148007936 | bytes 19922944 | tf_op jit(solution)/shard_map/dot_general | solution.py:17
  603.4 129.5 %all-reduce.17 = bf16[128,2048]{1,0:T(8,128)(2,1)} all-reduce(f32[128,2048]{1,0:T(8,128)S(1)} %fusion.1), channel_id=1, replica_groups=mesh['sample'=4,'marker'=32] {'marker'}, use_global_device_ids=true, to_apply=%region_12.0 | all-reduce | flops 262144 | bytes 1572864 | tf_op jit(solution)/shard_map/psum | solution.py:24
  732.9 9.6 %fusion.23 = f32[128,4096]{1,0:T(8,128)} fusion(bf16[128,2048]{1,0:T(8,128)(2,1)} %all-reduce.17, bf16[2048,4096]{1,0:T(8,128)(2,1)} %param.8), kind=kOutput, calls=%fused_computation.51 | convolution fusion | flops 2147483648 | bytes 19398656 | tf_op jit(solution)/shard_map/dot_general | solution.py:29
  742.7 58.7 %all-reduce.15.cloned.1.call-done = f32[128,4096]{1,0:T(8,128)} async-done(((f32[128,4096]{1,0:T(8,128)}), f32[128,4096]{1,0:T(8,128)}) %all-reduce.15.cloned.1.call-update) | async-done | bytes 2097168 | tf_op jit(solution)/shard_map/psum | solution.py:58
  801.3 2.7 multiply_reduce_fusion
  804.1 62.9 %psum.94 = f32[128]{0:T(128)S(1)} all-reduce(f32[128]{0:T(128)S(1)} %multiply_reduce_fusion), channel_id=1, replica_groups=mesh['sample'=4,'marker'=32] {'marker'}, use_global_device_ids=true, to_apply=%region_15.0 | all-reduce | flops 128 | bytes 1024 | tf_op jit(solution)/shard_map/psum | solution.py:60
  866.9 2.0 multiply_add_fusion
  868.9 1.3 copy-done.1
  870.3 0.3 fusion
  870.7 66.8 %psum.95 = f32[16]{0:T(128)S(1)} all-reduce(f32[16]{0:T(128)S(1)} %reduce_sum.78), channel_id=1, replica_groups=mesh['sample'=4,'marker'=32] {'marker'}, use_global_device_ids=true, to_apply=%region_18.0 | all-reduce | flops 16 | bytes 128 | tf_op jit(solution)/shard_map/psum | solution.py:73
  937.5 2.0 fusion.16
  (36 shorter events, 0.7 us)
Async XLA Ops:
  7.2 181.9 %all-reduce.9.cloned.1.call-start = ((), (), s32[]{:S(2)}) async-start(), calls=%async_computation | async-start | bytes 262144 | tf_op jit(solution)/shard_map/psum | solution.py:24
  75.4 113.7 %copy-start.3 = (f32[16,2048]{1,0:T(8,128)S(1)}, f32[16,2048]{1,0:T(8,128)}, u32[]{:S(2)}) copy-start(f32[16,2048]{1,0:T(8,128)} %param.9) | copy-start | bytes 393220
  86.3 111.6 %copy-start.6 = (f32[16]{0:T(128)S(1)}, f32[16]{0:T(128)}, u32[]{:S(2)}) copy-start(f32[16]{0:T(128)} %param.15) | copy-start | bytes 196
  86.3 152.5 %copy-start = (f32[112,4096]{1,0:T(8,128)S(1)}, f32[112,4096]{1,0:T(8,128)}, u32[]{:S(2)}) copy-start(f32[112,4096]{1,0:T(8,128)} %param.11) | copy-start | bytes 5505028
  86.4 151.4 %all-reduce.11.cloned.1.call-start = ((), (), s32[]{:S(2)}) async-start(), calls=%async_computation.1 | async-start | bytes 524288 | tf_op jit(solution)/shard_map/psum | solution.py:47
  197.9 255.7 %all-reduce.13.cloned.1.call-start = ((), (), s32[]{:S(2)}) async-start(), calls=%async_computation.2 | async-start | bytes 4194304 | tf_op jit(solution)/shard_map/psum | solution.py:58
  393.9 407.5 %all-reduce.15.cloned.1.call-start = ((), (), s32[]{:S(2)}) async-start(), calls=%async_computation.3 | async-start | bytes 4194304 | tf_op jit(solution)/shard_map/psum | solution.py:58
  868.9 1.4 copy-start.1
  870.3 67.2 %copy-start.4 = (f32[16]{0:T(128)S(1)}, f32[16]{0:T(128)}, u32[]{:S(2)}) copy-start(f32[16]{0:T(128)} %param.13) | copy-start | bytes 196
  870.3 67.2 %copy-start.5 = (f32[16]{0:T(128)S(1)}, f32[16]{0:T(128)}, u32[]{:S(2)}) copy-start(f32[16]{0:T(128)} %param.14) | copy-start | bytes 196
  870.3 67.2 %copy-start.2 = (f32[16,4096]{1,0:T(8,128)S(1)}, f32[16,4096]{1,0:T(8,128)}, u32[]{:S(2)}) copy-start(f32[16,4096]{1,0:T(8,128)} %param.10) | copy-start | bytes 786436
Sparse Core Ops, SparseCore 0:
  86.5 102.5 all-reduce.8
  198.1 39.6 all-reduce.10
  394.0 59.5 all-reduce.12
  742.6 58.6 all-reduce.14
where the time goes:
time: 947 us; the launch traced here: 946 us
  blocking collectives  587 us (62%)
  waiting for transfers between devices  261 us (28%)
  matrix products  62.4 us (7%)
  other arithmetic  20.5 us (2%)
  between operations  13.9 us (1%)
    psum x2, blocking collectives, project(): predicted = lax.psum(partial_value, 'marker')  264 us
    psum x2, waiting for transfers between devices, per_device(): back_sum = lax.psum(back_sum, 'sample')  118 us
    psum x1, waiting for transfers between devices, project(): predicted = lax.psum(partial_value, 'marker')  103 us
    psum x1, blocking collectives, per_device(): norm_next = lax.psum(jnp.sum(residual * residual, axis=1), 'marker')  66.8 us
    psum x1, blocking collectives, per_device(): probe_dot = lax.psum(probe_local, 'marker')  66.8 us
    psum x1, blocking collectives, per_device(): first_slope = lax.psum(jnp.sum(slopes, axis=1), 'marker') / MARKERS  63.8 us
    psum x1, blocking collectives, per_device(): curvature = lax.psum(jnp.sum(direction * applied, axis=1), 'marker')  62.9 us
    psum x1, blocking collectives, per_device(): norm_start = lax.psum(jnp.sum(residual * residual, axis=1), 'marker')  62.9 us
  transfers between devices with their start and end apart: 4, of which 4 were waited for; matrix products, arithmetic and copies ran while one was open for 0% of the time, Pallas kernels for 0%

commit v1 on v0

--- a/solution.py
+++ b/solution.py
@@ -62,7 +62,9 @@
         iterate = iterate + step_size[:, None] * direction
         if iteration + 1 < ITERS:
             residual = residual - step_size[:, None] * applied
-            norm_next = lax.psum(jnp.sum(residual * residual, axis=1), "marker")
+            norm_next = jnp.sum(
+                lax.all_gather(jnp.sum(residual * residual, axis=1), "marker"), axis=0
+            )
             beta_ratio = norm_next / norm_now
             direction = residual + beta_ratio[:, None] * direction
             norm_now = norm_next

time: 947 us -> 904 us (0.955)
  blocking collectives: 587 us -> 544 us
    psum x1 -> x0, blocking collectives: 66.8 us -> none  [per_device(): norm_next = lax.psum(jnp.sum(residual * residual, axis=1), 'marker')]
    all_gather x0 -> x1, blocking collectives: none -> 22.1 us  [per_device(): lax.all_gather(jnp.sum(residual * residual, axis=1), 'marker')]
where the time goes in v1:
time: 904 us
  blocking collectives  544 us (60%)
  waiting for transfers between devices  261 us (29%)
  matrix products  62.4 us (7%)
  other arithmetic  20.5 us (2%)
  between operations  13.9 us (2%)
    psum x2, blocking collectives, project(): predicted = lax.psum(partial_value, 'marker')  266 us
    psum x2, waiting for transfers between devices, per_device(): back_sum = lax.psum(back_sum, 'sample')  118 us
    psum x1, waiting for transfers between devices, project(): predicted = lax.psum(partial_value, 'marker')  103 us
    psum x1, blocking collectives, per_device(): probe_dot = lax.psum(probe_local, 'marker')  66.8 us
    psum x1, blocking collectives, per_device(): first_slope = lax.psum(jnp.sum(slopes, axis=1), 'marker') / MARKERS  63.8 us
    psum x1, blocking collectives, per_device(): curvature = lax.psum(jnp.sum(direction * applied, axis=1), 'marker')  62.9 us
    psum x1, blocking collectives, per_device(): norm_start = lax.psum(jnp.sum(residual * residual, axis=1), 'marker')  62.9 us
    psum x1, waiting for transfers between devices, per_device(): start_back = lax.psum(start_back, 'sample')  39.8 us
  transfers between devices with their start and end apart: 4, of which 4 were waited for; matrix products, arithmetic and copies ran while one was open for 0% of the time, Pallas kernels for 0%

profile of v1, /device:TPU:1, one launch (start us, length us, event | category | flops | bytes accessed | tf_op | source)
XLA Modules:
  0.0 903.6 jit_solution(5767118933144338933)
XLA Ops:
  7.2 0.7 multiply_add_fusion.4
  7.9 0.7 mul.192
  8.6 1.3 multiply_reduce_fusion.4
  9.8 63.8 %psum.77 = f32[16]{0:T(128)S(1)} all-reduce(f32[16]{0:T(128)S(1)} %multiply_reduce_fusion.4), channel_id=1, replica_groups=mesh['sample'=4,'marker'=32] {'marker'}, use_global_device_ids=true, to_apply=%region_1.0 | all-reduce | flops 16 | bytes 128 | tf_op jit(solution)/shard_map/psum | solution.py:43
  73.6 0.7 multiply_divide_fusion.1
  74.3 1.1 subtract_divide_fusion
  75.4 10.9 %fusion.17 = f32[16,2048]{1,0:T(8,128)} fusion(bf16[2048,4096]{1,0:T(8,128)(2,1)} %param.8, f32[16,4096]{1,0:T(8,128)S(1)} %subtract_divide_fusion), kind=kOutput, calls=%fused_computation.33 | convolution fusion | flops 268500992 | bytes 17170432 | tf_op jit(solution)/shard_map/dot_general | solution.py:17
  86.4 102.7 %all-reduce.9.cloned.1.call-done = f32[16,2048]{1,0:T(8,128)} async-done(((f32[16,2048]{1,0:T(8,128)}), f32[16,2048]{1,0:T(8,128)}) %all-reduce.9.cloned.1.call-update) | async-done | bytes 131088 | tf_op jit(solution)/shard_map/psum | solution.py:24
  189.1 8.8 fusion.19
  198.0 39.8 %all-reduce.11.cloned.1.call-done = f32[16,4096]{1,0:T(8,128)} async-done(((f32[16,4096]{1,0:T(8,128)}), f32[16,4096]{1,0:T(8,128)}) %all-reduce.11.cloned.1.call-update) | async-done | bytes 262160 | tf_op jit(solution)/shard_map/psum | solution.py:47
  237.8 1.0 broadcast_multiply_fusion
  238.8 11.4 %fusion.3 = f32[128,2048]{1,0:T(8,128)S(1)} fusion(bf16[2048,4096]{1,0:T(8,128)(2,1)} %param.8, f32[112,4096]{1,0:T(8,128)S(1)} %copy-done, f32[16,4096]{1,0:T(8,128)S(1)} %broadcast_multiply_fusion), kind=kOutput, calls=%fused_computation.13 | convolution fusion | flops 2149580800 | bytes 19922944 | tf_op jit(solution)/shard_map/dot_general | solution.py:17
  250.2 134.0 %all-reduce.16 = bf16[128,2048]{1,0:T(8,128)(2,1)} all-reduce(f32[128,2048]{1,0:T(8,128)S(1)} %fusion.3), channel_id=1, replica_groups=mesh['sample'=4,'marker'=32] {'marker'}, use_global_device_ids=true, to_apply=%region_6.0 | all-reduce | flops 262144 | bytes 1572864 | tf_op jit(solution)/shard_map/psum | solution.py:24
  384.2 9.6 %fusion.24 = f32[128,4096]{1,0:T(8,128)} fusion(bf16[128,2048]{1,0:T(8,128)(2,1)} %all-reduce.16, bf16[2048,4096]{1,0:T(8,128)(2,1)} %param.8), kind=kOutput, calls=%fused_computation.52 | convolution fusion | flops 2147483648 | bytes 19398656 | tf_op jit(solution)/shard_map/dot_general | solution.py:29
  394.0 0.1 mul.207
  394.1 59.5 %all-reduce.13.cloned.1.call-done = f32[128,4096]{1,0:T(8,128)} async-done(((f32[128,4096]{1,0:T(8,128)}), f32[128,4096]{1,0:T(8,128)}) %all-reduce.13.cloned.1.call-update) | async-done | bytes 2097168 | tf_op jit(solution)/shard_map/psum | solution.py:58
  453.6 2.2 multiply_reduce_fusion.2
  455.8 62.9 %all-reduce.1 = (f32[128]{0:T(128)S(1)}, f32[128]{0:T(128)S(1)}) all-reduce(f32[128]{0:T(128)S(1)} %get-tuple-element.3, f32[128]{0:T(128)S(1)} %get-tuple-element.2), channel_id=1, replica_groups=mesh['sample'=4,'marker'=32] {'marker'}, use_global_device_ids=true, to_apply=%region_5.0 | all-reduce | flops 256 | bytes 2048 | tf_op jit(solution)/shard_map/psum | solution.py:54
  518.7 2.2 multiply_reduce_fusion.1
  520.9 22.1 %all-gather.1 = f32[32,1,128]{2,1,0:T(1,128)S(1)} all-gather(f32[1,1,128]{2,1,0:T(1,128)S(1)} %bitcast.9), channel_id=2, replica_groups=mesh['sample'=4,'marker'=32] {'marker'}, dimensions={0}, use_global_device_ids=true | all-gather | bytes 16896 | tf_op jit(solution)/shard_map/all_gather | solution.py:66
  543.0 3.6 multiply_add_fusion.1
  546.6 12.1 %fusion.1 = f32[128,2048]{1,0:T(8,128)S(1)} fusion(bf16[2048,4096]{1,0:T(8,128)(2,1)} %param.8, f32[128,4096]{1,0:T(8,128)} %multiply_add_fusion.1), kind=kOutput, calls=%fused_computation.11 | convolution fusion | flops 2148007936 | bytes 19922944 | tf_op jit(solution)/shard_map/dot_general | solution.py:17
  558.7 131.8 %all-reduce.17 = bf16[128,2048]{1,0:T(8,128)(2,1)} all-reduce(f32[128,2048]{1,0:T(8,128)S(1)} %fusion.1), channel_id=1, replica_groups=mesh['sample'=4,'marker'=32] {'marker'}, use_global_device_ids=true, to_apply=%region_12.0 | all-reduce | flops 262144 | bytes 1572864 | tf_op jit(solution)/shard_map/psum | solution.py:24
  690.5 9.6 %fusion.23 = f32[128,4096]{1,0:T(8,128)} fusion(bf16[128,2048]{1,0:T(8,128)(2,1)} %all-reduce.17, bf16[2048,4096]{1,0:T(8,128)(2,1)} %param.8), kind=kOutput, calls=%fused_computation.51 | convolution fusion | flops 2147483648 | bytes 19398656 | tf_op jit(solution)/shard_map/dot_general | solution.py:29
  700.2 58.7 %all-reduce.15.cloned.1.call-done = f32[128,4096]{1,0:T(8,128)} async-done(((f32[128,4096]{1,0:T(8,128)}), f32[128,4096]{1,0:T(8,128)}) %all-reduce.15.cloned.1.call-update) | async-done | bytes 2097168 | tf_op jit(solution)/shard_map/psum | solution.py:58
  758.9 2.7 multiply_reduce_fusion
  761.6 62.9 %psum.86 = f32[128]{0:T(128)S(1)} all-reduce(f32[128]{0:T(128)S(1)} %multiply_reduce_fusion), channel_id=1, replica_groups=mesh['sample'=4,'marker'=32] {'marker'}, use_global_device_ids=true, to_apply=%region_15.0 | all-reduce | flops 128 | bytes 1024 | tf_op jit(solution)/shard_map/psum | solution.py:60
  824.5 2.0 multiply_add_fusion
  826.5 1.3 copy-done.1
  827.9 0.3 fusion
  828.2 66.8 %psum.87 = f32[16]{0:T(128)S(1)} all-reduce(f32[16]{0:T(128)S(1)} %reduce_sum.88), channel_id=1, replica_groups=mesh['sample'=4,'marker'=32] {'marker'}, use_global_device_ids=true, to_apply=%region_18.0 | all-reduce | flops 16 | bytes 128 | tf_op jit(solution)/shard_map/psum | solution.py:75
  895.1 2.0 fusion.16
  (37 shorter events, 0.7 us)
Async XLA Ops:
  7.2 181.9 %all-reduce.9.cloned.1.call-start = ((), (), s32[]{:S(2)}) async-start(), calls=%async_computation | async-start | bytes 262144 | tf_op jit(solution)/shard_map/psum | solution.py:24
  75.4 113.7 %copy-start.3 = (f32[16,2048]{1,0:T(8,128)S(1)}, f32[16,2048]{1,0:T(8,128)}, u32[]{:S(2)}) copy-start(f32[16,2048]{1,0:T(8,128)} %param.9) | copy-start | bytes 393220
  86.3 111.6 %copy-start.6 = (f32[16]{0:T(128)S(1)}, f32[16]{0:T(128)}, u32[]{:S(2)}) copy-start(f32[16]{0:T(128)} %param.15) | copy-start | bytes 196
  86.3 152.5 %copy-start = (f32[112,4096]{1,0:T(8,128)S(1)}, f32[112,4096]{1,0:T(8,128)}, u32[]{:S(2)}) copy-start(f32[112,4096]{1,0:T(8,128)} %param.11) | copy-start | bytes 5505028
  86.4 151.4 %all-reduce.11.cloned.1.call-start = ((), (), s32[]{:S(2)}) async-start(), calls=%async_computation.1 | async-start | bytes 524288 | tf_op jit(solution)/shard_map/psum | solution.py:47
  197.9 255.7 %all-reduce.13.cloned.1.call-start = ((), (), s32[]{:S(2)}) async-start(), calls=%async_computation.2 | async-start | bytes 4194304 | tf_op jit(solution)/shard_map/psum | solution.py:58
  393.9 365.0 %all-reduce.15.cloned.1.call-start = ((), (), s32[]{:S(2)}) async-start(), calls=%async_computation.3 | async-start | bytes 4194304 | tf_op jit(solution)/shard_map/psum | solution.py:58
  826.5 1.4 copy-start.1
  827.8 67.2 %copy-start.4 = (f32[16]{0:T(128)S(1)}, f32[16]{0:T(128)}, u32[]{:S(2)}) copy-start(f32[16]{0:T(128)} %param.13) | copy-start | bytes 196
  827.9 67.2 %copy-start.5 = (f32[16]{0:T(128)S(1)}, f32[16]{0:T(128)}, u32[]{:S(2)}) copy-start(f32[16]{0:T(128)} %param.14) | copy-start | bytes 196
  827.9 67.2 %copy-start.2 = (f32[16,4096]{1,0:T(8,128)S(1)}, f32[16,4096]{1,0:T(8,128)}, u32[]{:S(2)}) copy-start(f32[16,4096]{1,0:T(8,128)} %param.10) | copy-start | bytes 786436
Sparse Core Ops, SparseCore 0:
  86.5 102.5 all-reduce.8
  198.1 39.6 all-reduce.10
  394.0 59.5 all-reduce.12
  700.2 58.6 all-reduce.14
